TPU v7x, 512 devices: a whole 4x4x16 slice. The times are simulated.
512 devices in a mesh: section: 4 (over x_hi, core), row: 128 (over z, x_lo, y).
Axes of the slice: x: 4 (x_hi: 2, x_lo: 2; x = x_hi * 2 + x_lo), y: 4, z: 16, core: 2. Of those that a mesh axis runs over, the one named last changes fastest.
Arguments:
- layer_input: bfloat16 [4, 16384, 4096], P('section', 'row'), may hold values from -6 to 6
- cotangent: bfloat16 [4, 16384, 4096], P('section', 'row'), may hold values from -6 to 6
- route_weight: float32 [4, 16384, 2], P('section', 'row'), may hold values from 0.1 to 0.9
- chosen: int32 [4, 16384, 2], P('section', 'row'), may hold values from 0 to 7, all different within a row
- hot_expert: int32 [4], P('section'), may hold values from 0 to 7
- store_in: bfloat16 [4, 2, 4096, 7168], P('section', None, None, 'row'), may hold values from -0.09375 to 0.09375
- store_out: bfloat16 [4, 7168, 4096], P('section', 'row'), may hold values from -0.0625 to 0.0625
Outputs:
- back_cot: bfloat16 [4, 16384, 4096], P('section', 'row')
- route_grad: float32 [4, 16384, 2], P('section', 'row')
Inputs may be any that keep to these rules, and one draw needn't show every extreme that they name: `chosen`: each token names 2 different experts.
All inputs are finite; a program needn't handle non-finite values.
Results may differ from a plain program's by a relative error of at most 0.0034.
Values may be sent and summed in bfloat16 or wider, within the bound.
No kernel may reach another device: no remote copies, remote signals or barrier semaphores. Data moves between devices by JAX's collectives and lax.ppermute only.
A program may use at most 64 MiB of HBM per device.

v0:
```python
import jax
import jax.numpy as jnp
from jax import lax
from jax.experimental import pallas as pl
from jax.experimental.pallas import tpu as pltpu
from jax.sharding import PartitionSpec as P


CAP = 2
TOP = 2
PLANE = 8
SENT_DOWN = 32
PAD = 128
NONE = 128

bf16 = jnp.bfloat16
f32 = jnp.float32


def slot_tokens(chosen, hot):
    hit = chosen == hot
    lane = lax.broadcasted_iota(jnp.int32, hit.shape, 1)
    at = jnp.where(hit, lane, NONE)
    first = jnp.min(jnp.min(at, axis=1, keepdims=True), axis=0, keepdims=True)
    later = jnp.where(at > first, at, NONE)
    second = jnp.min(jnp.min(later, axis=1, keepdims=True), axis=0, keepdims=True)
    return hit, lane, first, second


def total(values):
    return jnp.sum(jnp.sum(values, axis=1, keepdims=True), axis=0, keepdims=True)


def select_kernel(
    chosen_hbm, hot_ref, weight_hbm, x_hbm, g_hbm,
    sent_ref, cot_ref, w_ref, t_ref, held_ref,
    chosen_ref, weight_ref, x_ref, g_ref, sems,
):
    pairs = (
        (chosen_hbm, chosen_ref),
        (weight_hbm, weight_ref),
        (x_hbm, x_ref),
        (g_hbm, g_ref),
    )
    coming = [pltpu.make_async_copy(src, dst, sems.at[i]) for i, (src, dst) in enumerate(pairs)]
    for copy in coming:
        copy.start()
    for copy in coming[:2]:
        copy.wait()
    hit, lane, first, second = slot_tokens(chosen_ref[...], hot_ref[0])
    weights = weight_ref[...]
    in_first, in_second = hit & (lane == first), hit & (lane == second)
    held_ref[...] = jnp.zeros_like(held_ref)
    held_ref[0:2] = in_first.astype(f32)
    held_ref[4:6] = in_second.astype(f32)
    w_first = total(jnp.where(in_first, weights, 0.0))
    w_second = total(jnp.where(in_second, weights, 0.0))
    tokens = x_ref.shape[0]
    row = lax.broadcasted_iota(jnp.int32, (8, tokens), 0)
    col = lax.broadcasted_iota(jnp.int32, (8, tokens), 1)
    token = jnp.where(row < 4, first, second)
    pick = (col == token).astype(f32).astype(bf16)
    t_ref[...] = token.astype(f32)
    w_ref[...] = jnp.where(row < 4, w_first, w_second)
    for copy in coming[2:]:
        copy.wait()
    x_rows = jnp.dot(pick, x_ref[...], preferred_element_type=f32)
    g_rows = jnp.dot(pick, g_ref[...], preferred_element_type=f32)
    half = x_rows.shape[1] // 2
    quarter = half // 2
    at = lax.broadcasted_iota(jnp.int32, (8, half), 0)
    low = (at & 2) == 0
    unit = jnp.where(
        (at & 1) == 0,
        jnp.where(low, x_rows[:, :half], x_rows[:, half:]),
        jnp.where(low, g_rows[:, :half], g_rows[:, half:]),
    ).astype(bf16)
    for i in range(sent_ref.shape[0]):
        sent_ref[i] = unit
    at = lax.broadcasted_iota(jnp.int32, (8, quarter), 0) & 3
    cot = g_rows[:, :quarter]
    for q in range(1, 4):
        cot = jnp.where(at == q, g_rows[:, q * quarter : (q + 1) * quarter], cot)
    cot_ref[...] = cot


def weights_kernel(in_ref, out_ref, below_ref, above_ref, w_all):
    width, own = in_ref.shape[2], in_ref.shape[1]
    n_above, n_below = above_ref.shape[1], below_ref.shape[1]
    for kind in range(3):
        at = kind * PAD
        w_all[at + 48 : at + 64, :] = jnp.zeros((16, width), bf16)
        w_all[at + 112 : at + 128, :] = jnp.zeros((16, width), bf16)
        w_all[at : at + n_above, :] = above_ref[kind]
        w_all[at + n_above : at + n_above + n_below, :] = below_ref[kind]
        w_all[at + 64 : at + 64 + own, :] = in_ref[kind] if kind < 2 else out_ref[...]


def spread_kernel(column_ref, sent_ref, sems):
    copies = [
        pltpu.make_async_copy(column_ref, sent_ref.at[i], sems.at[i]) for i in range(sent_ref.shape[0])
    ]
    for copy in copies:
        copy.start()
    for copy in copies:
        copy.wait()


def expert_kernel(rows_hbm, w_all, _, part_ref, rows_ref, prod, wide, in_sems):
    width = w_all.shape[1]
    half, quarter = width // 2, width // 4
    count = rows_ref.shape[0] // 4
    pieces = in_sems.shape[0]
    height = rows_ref.shape[0] // pieces
    coming = []
    for i in range(pieces):
        at = slice(i * height, (i + 1) * height)
        coming.append(pltpu.make_async_copy(rows_hbm.at[at], rows_ref.at[at], in_sems.at[i]))
        coming[i].start()
    nt = (((1,), (1,)), ((), ()))
    for i in range(pieces):
        at = slice(i * height, (i + 1) * height)
        coming[i].wait()
        for h in range(2):
            cols = slice(h * half, (h + 1) * half)
            out = lax.dot_general(
                rows_ref[at, :],
                w_all[:, cols],
                nt,
                preferred_element_type=f32,
            )
            for column in range(3):
                prod[h * 3 + column, at, :] = out[:, column * PAD : (column + 1) * PAD]

    def taken(kind, column):
        low = prod[column, pl.ds(kind, count, stride=4), :]
        return low + prod[3 + column, pl.ds(2 + kind, count, stride=4), :]

    gate, upper, d_hidden = taken(0, 0), taken(0, 1), taken(1, 2)
    sig = 1.0 / (1.0 + jnp.exp(-gate))
    hidden = (gate * sig * upper).astype(bf16)
    d_gate = (d_hidden * upper * sig * (1.0 + gate * (1.0 - sig))).astype(bf16)
    d_up = (d_hidden * gate * sig).astype(bf16)
    score = jnp.sum(hidden.astype(f32) * d_hidden, axis=1, keepdims=True)
    both = jnp.concatenate([d_gate, d_up], axis=1)
    peers, tall = part_ref.shape[0], rows_ref.shape[0] // part_ref.shape[0]
    blocks = quarter // 128
    part_ref[:, blocks * tall :, :] = score_pieces(score).reshape(peers, tall // 4, 128).astype(bf16)
    for at in range(0, blocks, 2):
        for q in range(4):
            cols = slice(q * quarter + at * 128, q * quarter + (at + 2) * 128)
            back = jnp.dot(both, w_all[: 2 * PAD, cols], preferred_element_type=f32)
            wide[at, pl.ds(q, count, stride=4), :] = back[:, :128]
            wide[at + 1, pl.ds(q, count, stride=4), :] = back[:, 128:]
        for i in (at, at + 1):
            part_ref[:, i * tall : (i + 1) * tall, :] = wide[i].reshape(peers, tall, 128).astype(bf16)


def score_pieces(score):
    lane = lax.broadcasted_iota(jnp.int32, (score.shape[0], 128), 1)
    rest = jnp.broadcast_to(score, lane.shape)
    out = jnp.zeros_like(rest)
    for i in range(3):
        piece = rest.astype(bf16).astype(f32)
        out = jnp.where(lane == i, piece, out)
        rest = rest - piece
    return out


def summed(got_ref):
    acc = got_ref[0].astype(f32)
    for i in range(1, got_ref.shape[0]):
        acc = acc + got_ref[i].astype(f32)
    return acc


def middle_kernel(got_ref, cot_hbm, part_ref, cot_ref, tile, scores, sem):
    copy = pltpu.make_async_copy(cot_hbm, cot_ref, sem)
    copy.start()
    peers = part_ref.shape[0]
    tall = peers * 8
    acc = summed(got_ref)
    blocks = (acc.shape[0] - tall // 4) // tall
    for i in range(blocks):
        rows = acc[i * tall : (i + 1) * tall].reshape(peers, 8, 128)
        part_ref[:, i * 8 : (i + 1) * 8, :] = rows.astype(bf16)
    scores[...] = score_pieces(jnp.sum(acc[blocks * tall :], axis=1, keepdims=True))
    tile[...] = jnp.zeros_like(tile)
    for a in range(peers):
        tile[a, 0:CAP] = scores[CAP * a : CAP * (a + 1)]
    part_ref[:, blocks * 8 :, :] = tile[...].astype(bf16)
    copy.wait()


def last_kernel(got_ref, cot_ref, w_ref, t_ref, held_ref, moved_ref, grad_ref):
    acc = summed(got_ref)
    quarter = cot_ref.shape[1]
    w = w_ref[...]
    for i in range(quarter // 128):
        cols = slice(i * 128, (i + 1) * 128)
        back = acc[i * 8 : (i + 1) * 8].astype(bf16).astype(f32)
        moved_ref[:, cols] = (cot_ref[:, cols] + w * back).astype(bf16)
    moved_ref[:, quarter:] = t_ref[...].astype(bf16)
    score = jnp.sum(acc[quarter // 16 :], axis=1, keepdims=True)
    grad_ref[...] = held_ref[0:2] * score[0:1] + held_ref[4:6] * score[1:2]


def place_kernel(cot_ref, moved_ref, out_ref, ready, sems):
    tokens, width = cot_ref.shape
    quarter = width // 4
    row = lax.broadcasted_iota(jnp.int32, (tokens, 128), 0).astype(f32)
    token = moved_ref[:, quarter:].astype(f32)
    at = [(row == token[4 * s : 4 * s + 1])[:, :1] for s in range(CAP)]
    copies = []
    for q in range(4):
        cols = slice(q * quarter, (q + 1) * quarter)
        value = cot_ref[:, cols].astype(f32)
        for s in range(CAP):
            value = jnp.where(at[s], moved_ref[4 * s + q : 4 * s + q + 1, :quarter].astype(f32), value)
        ready[:, cols] = value.astype(bf16)
        copies.append(pltpu.make_async_copy(ready.at[:, cols], out_ref.at[:, cols], sems.at[q]))
        copies[q].start()
    for copy in copies:
        copy.wait()


def call(kernel, outs, *operands, scratch=(), smem=(), near=(), far=(), out_space=pltpu.VMEM):
    def placed(i, v):
        if i in near or i in far:
            return pltpu.with_memory_space_constraint(v, pltpu.VMEM if i in near else pltpu.HBM)
        return v

    def space(i):
        return pltpu.SMEM if i in smem else pltpu.HBM if i in far else pltpu.VMEM

    return pl.pallas_call(
        kernel,
        out_shape=outs,
        in_specs=[pl.BlockSpec(memory_space=space(i)) for i in range(len(operands))],
        out_specs=[pl.BlockSpec(memory_space=out_space)] * len(outs),
        scratch_shapes=list(scratch),
        compiler_params=pltpu.CompilerParams(vmem_limit_bytes=24 << 20),
    )(*(placed(i, v) for i, v in enumerate(operands)))


def shape(dims, kind):
    return jax.ShapeDtypeStruct(dims, kind)


def on_device(layer_input, cotangent, route_weight, chosen, hot_expert, store_in, store_out):
    tokens, width = layer_input.shape[1:]
    half, quarter = width // 2, width // 4
    num_row = lax.axis_size("row")
    heights = num_row // PLANE
    peers = heights // 2
    along_z = [[a * 2 * PLANE + r for a in range(peers)] for r in range(2 * PLANE)]
    in_plane = [[z * PLANE + i for i in range(PLANE)] for z in range(heights)]
    sections = lax.axis_size("section")
    back_one = [(i, i - 1) for i in range(1, sections)]

    def exchange(value, groups):
        return lax.all_to_all(
            value, "row", split_axis=0, concat_axis=0, axis_index_groups=groups, tiled=True
        )

    def along(value, by):
        return lax.ppermute(value, "row", [(i, (i + by * PLANE) % num_row) for i in range(num_row)])

    w_in = jnp.swapaxes(store_in[0], 1, 2)
    w_out = store_out[0]
    w_both = jnp.concatenate([w_in, w_out[None]], axis=0)
    from_above = along(w_both[:, :SENT_DOWN], -1)
    from_below = along(w_both[:, SENT_DOWN:], 1)
    cot_moved = lax.ppermute(cotangent[0], "section", back_one)

    unit, cot_rows, w_rows, t_rows, held = call(
        select_kernel,
        [
            pltpu.VMEM((peers, 8, half), bf16),
            pltpu.VMEM((8, quarter), f32),
            pltpu.VMEM((8, tokens), f32),
            pltpu.VMEM((8, tokens), f32),
            pltpu.VMEM((8, tokens), f32),
        ],
        chosen[0].T,
        hot_expert,
        route_weight[0].T,
        layer_input[0],
        cotangent[0],
        scratch=(
            pltpu.VMEM((TOP, tokens), jnp.int32),
            pltpu.VMEM((TOP, tokens), f32),
            pltpu.VMEM((tokens, width), bf16),
            pltpu.VMEM((tokens, width), bf16),
            pltpu.SemaphoreType.DMA((4,)),
        ),
        smem=(1,),
        far=(0, 2, 3, 4),
    )
    tall = peers * 8
    column = exchange(unit, along_z).reshape(tall, half)
    (sent,) = call(
        spread_kernel,
        [pltpu.HBM((PLANE, tall, half), bf16)],
        column,
        scratch=(pltpu.SemaphoreType.DMA((PLANE,)),),
        near=(0,),
        out_space=pltpu.HBM,
    )
    rows = exchange(sent, in_plane)
    (w_all,) = call(
        weights_kernel,
        [pltpu.VMEM((3 * PAD, width), bf16)],
        w_in,
        w_out,
        from_below,
        from_above,
        near=(0, 1, 2, 3),
    )
    count = PLANE * tall
    (part,) = call(
        expert_kernel,
        [pltpu.VMEM((PLANE, quarter // 128 * tall + tall // 4, 128), bf16)],
        rows.reshape(count, half),
        w_all,
        cot_moved,
        scratch=(
            pltpu.VMEM((count, half), bf16),
            pltpu.VMEM((6, count, PAD), f32),
            pltpu.VMEM((quarter // 128, count, 128), f32),
            pltpu.SemaphoreType.DMA((4,)),
        ),
        near=(1,),
        far=(0, 2),
    )
    got = exchange(part, in_plane)
    part, cot_moved = call(
        middle_kernel,
        [pltpu.VMEM((peers, quarter // 16 + 8, 128), bf16), pltpu.VMEM((tokens, width), bf16)],
        got,
        cot_moved,
        scratch=(
            pltpu.VMEM((peers, 8, 128), f32),
            pltpu.VMEM((peers * CAP, 128), f32),
            pltpu.SemaphoreType.DMA,
        ),
        near=(0,),
        far=(1,),
    )
    got = exchange(part, along_z)
    moved, grad = call(
        last_kernel,
        [pltpu.VMEM((8, quarter + 128), bf16), shape((TOP, tokens), f32)],
        got,
        cot_rows,
        w_rows,
        t_rows,
        held,
        near=(0, 1, 2, 3, 4),
    )
    moved = lax.ppermute(moved, "section", back_one)
    (back_cot,) = call(
        place_kernel,
        [pltpu.HBM((tokens, width), bf16)],
        cot_moved,
        moved,
        scratch=(pltpu.VMEM((tokens, width), bf16), pltpu.SemaphoreType.DMA((4,))),
        near=(0, 1),
        out_space=pltpu.HBM,
    )
    return (back_cot[None], grad.T[None])


def solution(mesh):
    in_specs = (
        P("section", "row", None),
        P("section", "row", None),
        P("section", "row", None),
        P("section", "row", None),
        P("section"),
        P("section", None, None, "row"),
        P("section", "row", None),
    )
    out_specs = (P("section", "row", None), P("section", "row", None))

    return jax.shard_map(on_device, mesh=mesh, in_specs=in_specs, out_specs=out_specs, check_vma=False)
```

profile of v0, /device:TPU:1, one launch (start us, length us, event | category | flops | bytes accessed | tf_op | source)
XLA Modules:
  0.0 131.5 jit_solution(3424941531067737193)
XLA Ops:
  1.3 2.0 %shard_map.86 = (bf16[8,8,2048]{2,1,0:T(8,128)(2,1)S(1)}, f32[8,1024]{1,0:T(8,128)S(1)}, f32[8,128]{1,0:T(8,128)S(1)}, f32[8,128]{1,0:T(8,128)S(1)}, f32[8,128]{1,0:T(8,128)S(1)}) custom-call(s32[2,128]{1,0:T(2,128)} %bitcast.25, s32[1]{0:T(128)S(6)} %copy.9.hot_ref, f32[2,128]{1,0:T(2,128)} %bitcast.26, bf16[128,4096]{1,0:T(8,128)(2,1)} %bitcast.24, ...), custom_call_target="tpu_custom_call" | custom-call | tf_op jit(solution)/shard_map/pallas_call | solution.py:236
  3.3 32.7 %all_to_all.20 = bf16[8,8,2048]{2,1,0:T(8,128)(2,1)S(1)} all-to-all(bf16[8,8,2048]{2,1,0:T(8,128)(2,1)S(1)} %get-tuple-element.11), channel_id=1, replica_groups={{0,16,32,48,64,80,96,112},{1,17,33,49,65,81,97,113},{2,18,34,50,66,82,9..., dimensions={0} | all-to-all | bytes 524288 | tf_op jit(solution)/shard_map/all_to_all | solution.py:262
  36.0 1.4 %shard_map.87 = bf16[8,64,2048]{2,1,0:T(8,128)(2,1)} custom-call(bf16[64,2048]{1,0:T(8,128)(2,1)S(1)} %bitcast.22), custom_call_target="tpu_custom_call" | custom-call | tf_op jit(solution)/shard_map/pallas_call | solution.py:236
  37.4 0.0 copy-start
  37.4 0.0 copy-start.2
  37.4 5.3 %all-to-all-start.1 = ((bf16[8,64,2048]{2,1,0:T(8,128)(2,1)}), bf16[8,64,2048]{2,1,0:T(8,128)(2,1)}, u32[]{:S(2)}, u32[]{:S(2)}) async-start(bf16[8,64,2048]{2,1,0:T(8,128)(2,1)} %shard_map.87), calls=%async_computation.1 | async-start | bytes 4194304 | tf_op jit(solution)/shard_map/all_to_all | solution.py:262
  42.7 7.2 %collective-permute-start.2 = (bf16[128,4096]{1,0:T(8,128)(2,1)}, bf16[128,4096]{1,0:T(8,128)(2,1)}, u32[]{:S(2)}, u32[]{:S(2)}) collective-permute-start(bf16[128,4096]{1,0:T(8,128)(2,1)} %bitcast.5.g_hbm), channel_id=1, source_target_pairs={{128,0},{256,128},{384,256},{129,1},{257,129},{385,257},{130,2},{2... | collective-permute-start | bytes 3145736 | tf_op jit(solution)/shard_map/ppermute | solution.py:274
  49.9 0.0 copy-done
  49.9 0.0 copy-done.2
  49.9 0.0 copy-start.1
  49.9 0.0 copy-start.3
  49.9 0.1 pad_maximum_fusion
  50.0 2.1 %collective-permute-start.1 = (bf16[3,32,4096]{2,1,0:T(8,128)(2,1)S(1)}, bf16[3,32,4096]{2,1,0:T(8,128)(2,1)S(1)}, u32[]{:S(2)}, u32[]{:S(2)}) collective-permute-start(bf16[3,32,4096]{2,1,0:T(8,128)(2,1)S(1)} %pad_maximum_fusion), channel_id=1, source_target_pairs={{0,120},{1,121},{2,122},{3,123},{4,124},{5,125},{6,126},{7,127},{8... | collective-permute-start | bytes 2359304 | tf_op jit(solution)/shard_map/ppermute | solution.py:267
  52.1 3.4 %collective-permute-start = (bf16[3,24,4096]{2,1,0:T(8,128)(2,1)S(1)}, bf16[3,24,4096]{2,1,0:T(8,128)(2,1)S(1)}, u32[]{:S(2)}, u32[]{:S(2)}) collective-permute-start(bf16[3,24,4096]{2,1,0:T(8,128)(2,1)S(1)} %pad_maximum_fusion.1), channel_id=1, source_target_pairs={{0,8},{1,9},{2,10},{3,11},{4,12},{5,13},{6,14},{7,15},{8,16},{9,17... | collective-permute-start | bytes 1769480 | tf_op jit(solution)/shard_map/ppermute | solution.py:267
  55.5 14.8 %collective-permute-done.below_ref = bf16[3,24,4096]{2,1,0:T(8,128)(2,1)S(1)} collective-permute-done((bf16[3,24,4096]{2,1,0:T(8,128)(2,1)S(1)}, bf16[3,24,4096]{2,1,0:T(8,128)(2,1)S(1)}, u32[]{:S(2)}, u32[]{:S(2)}) %collective-permute-start) | collective-permute-done | bytes 589856 | tf_op jit(solution)/shard_map/ppermute | solution.py:267
  70.2 1.0 collective-permute-done.1.above_ref
  71.3 0.0 copy-done.1
  71.3 0.0 copy-done.3
  71.3 0.2 shard_map.88.w_all
  71.5 8.7 %collective-permute-done.2._.cot_hbm = bf16[128,4096]{1,0:T(8,128)(2,1)} collective-permute-done((bf16[128,4096]{1,0:T(8,128)(2,1)}, bf16[128,4096]{1,0:T(8,128)(2,1)}, u32[]{:S(2)}, u32[]{:S(2)}) %collective-permute-start.2) | collective-permute-done | bytes 1048608 | tf_op jit(solution)/shard_map/ppermute | solution.py:274
  80.2 0.0 all-to-all-done.1
  80.2 5.8 %shard_map.89 = bf16[8,528,128]{2,1,0:T(8,128)(2,1)S(1)} custom-call(bf16[512,2048]{1,0:T(8,128)(2,1)} %bitcast.7.rows_hbm, bf16[384,4096]{1,0:T(8,128)(2,1)S(1)} %shard_map.88.w_all, bf16[128,4096]{1,0:T(8,128)(2,1)} %collective-permute-done.2._.cot_hbm), custom_call_target="tpu_custom_call" | custom-call | tf_op jit(solution)/shard_map/pallas_call | solution.py:236
  86.0 15.1 %all_to_all.21.got_ref = bf16[8,528,128]{2,1,0:T(8,128)(2,1)S(1)} all-to-all(bf16[8,528,128]{2,1,0:T(8,128)(2,1)S(1)} %shard_map.89), channel_id=1, replica_groups={{0,1,2,3,4,5,6,7},{8,9,10,11,12,13,14,15},{16,17,18,19,20,21,22,23},{24..., dimensions={0} | all-to-all | bytes 2162688 | tf_op jit(solution)/shard_map/all_to_all | solution.py:262
  101.1 1.2 shard_map.90
  102.3 20.6 %all_to_all.22.got_ref = bf16[8,72,128]{2,1,0:T(8,128)(2,1)S(1)} all-to-all(bf16[8,72,128]{2,1,0:T(8,128)(2,1)S(1)} %get-tuple-element.13), channel_id=1, replica_groups={{0,16,32,48,64,80,96,112},{1,17,33,49,65,81,97,113},{2,18,34,50,66,82,9..., dimensions={0} | all-to-all | bytes 294912 | tf_op jit(solution)/shard_map/all_to_all | solution.py:262
  122.9 0.7 shard_map.91
  123.6 1.9 %collective-permute-start.3 = (bf16[8,1152]{1,0:T(8,128)(2,1)S(1)}, bf16[8,1152]{1,0:T(8,128)(2,1)S(1)}, u32[]{:S(2)}, u32[]{:S(2)}) collective-permute-start(bf16[8,1152]{1,0:T(8,128)(2,1)S(1)} %get-tuple-element.18), channel_id=1, source_target_pairs={{128,0},{256,128},{384,256},{129,1},{257,129},{385,257},{130,2},{2... | collective-permute-start | bytes 55304 | tf_op jit(solution)/shard_map/ppermute | solution.py:361
  125.5 4.7 %collective-permute-done.3.moved_ref = bf16[8,1152]{1,0:T(8,128)(2,1)S(1)} collective-permute-done((bf16[8,1152]{1,0:T(8,128)(2,1)S(1)}, bf16[8,1152]{1,0:T(8,128)(2,1)S(1)}, u32[]{:S(2)}, u32[]{:S(2)}) %collective-permute-start.3) | collective-permute-done | bytes 18464 | tf_op jit(solution)/shard_map/ppermute | solution.py:361
  130.2 1.3 shard_map.92
  (1 shorter events, 0.0 us)
Async XLA Ops:
  37.4 12.5 %copy-start = (bf16[1,2,4096,56]{2,3,1,0:T(8,128)(2,1)S(1)}, bf16[1,2,4096,56]{2,3,1,0:T(8,128)(2,1)}, u32[]{:S(2)}) copy-start(bf16[1,2,4096,56]{2,3,1,0:T(8,128)(2,1)} %param.12) | copy-start | bytes 2752516
  37.4 12.5 %copy-start.2 = (bf16[1,56,4096]{2,1,0:T(8,128)(2,1)S(1)}, bf16[1,56,4096]{2,1,0:T(8,128)(2,1)}, u32[]{:S(2)}) copy-start(bf16[1,56,4096]{2,1,0:T(8,128)(2,1)} %param.13) | copy-start | bytes 1376260
  37.4 42.8 %all-to-all-start.1 = ((bf16[8,64,2048]{2,1,0:T(8,128)(2,1)}), bf16[8,64,2048]{2,1,0:T(8,128)(2,1)}, u32[]{:S(2)}, u32[]{:S(2)}) async-start(bf16[8,64,2048]{2,1,0:T(8,128)(2,1)} %shard_map.87), calls=%async_computation.1 | async-start | bytes 4194304 | tf_op jit(solution)/shard_map/all_to_all | solution.py:262
  42.7 37.5 %collective-permute-start.2 = (bf16[128,4096]{1,0:T(8,128)(2,1)}, bf16[128,4096]{1,0:T(8,128)(2,1)}, u32[]{:S(2)}, u32[]{:S(2)}) collective-permute-start(bf16[128,4096]{1,0:T(8,128)(2,1)} %bitcast.5.g_hbm), channel_id=1, source_target_pairs={{128,0},{256,128},{384,256},{129,1},{257,129},{385,257},{130,2},{2... | collective-permute-start | bytes 3145736 | tf_op jit(solution)/shard_map/ppermute | solution.py:274
  49.9 21.4 %copy-start.1 = (bf16[1,2,4096,56]{2,3,1,0:T(8,128)(2,1)S(1)}, bf16[1,2,4096,56]{2,3,1,0:T(8,128)(2,1)}, u32[]{:S(2)}) copy-start(bf16[1,2,4096,56]{2,3,1,0:T(8,128)(2,1)} %param.12) | copy-start | bytes 2752516
  49.9 21.3 %copy-start.3 = (bf16[1,56,4096]{2,1,0:T(8,128)(2,1)S(1)}, bf16[1,56,4096]{2,1,0:T(8,128)(2,1)}, u32[]{:S(2)}) copy-start(bf16[1,56,4096]{2,1,0:T(8,128)(2,1)} %param.13) | copy-start | bytes 1376260
  50.0 21.3 %collective-permute-start.1 = (bf16[3,32,4096]{2,1,0:T(8,128)(2,1)S(1)}, bf16[3,32,4096]{2,1,0:T(8,128)(2,1)S(1)}, u32[]{:S(2)}, u32[]{:S(2)}) collective-permute-start(bf16[3,32,4096]{2,1,0:T(8,128)(2,1)S(1)} %pad_maximum_fusion), channel_id=1, source_target_pairs={{0,120},{1,121},{2,122},{3,123},{4,124},{5,125},{6,126},{7,127},{8... | collective-permute-start | bytes 2359304 | tf_op jit(solution)/shard_map/ppermute | solution.py:267
  52.1 18.1 %collective-permute-start = (bf16[3,24,4096]{2,1,0:T(8,128)(2,1)S(1)}, bf16[3,24,4096]{2,1,0:T(8,128)(2,1)S(1)}, u32[]{:S(2)}, u32[]{:S(2)}) collective-permute-start(bf16[3,24,4096]{2,1,0:T(8,128)(2,1)S(1)} %pad_maximum_fusion.1), channel_id=1, source_target_pairs={{0,8},{1,9},{2,10},{3,11},{4,12},{5,13},{6,14},{7,15},{8,16},{9,17... | collective-permute-start | bytes 1769480 | tf_op jit(solution)/shard_map/ppermute | solution.py:267
  123.6 6.6 %collective-permute-start.3 = (bf16[8,1152]{1,0:T(8,128)(2,1)S(1)}, bf16[8,1152]{1,0:T(8,128)(2,1)S(1)}, u32[]{:S(2)}, u32[]{:S(2)}) collective-permute-start(bf16[8,1152]{1,0:T(8,128)(2,1)S(1)} %get-tuple-element.18), channel_id=1, source_target_pairs={{128,0},{256,128},{384,256},{129,1},{257,129},{385,257},{130,2},{2... | collective-permute-start | bytes 55304 | tf_op jit(solution)/shard_map/ppermute | solution.py:361
where the time goes:
time: 132 us; the launch traced here: 131 us
  blocking collectives  68.4 us (52%)
  waiting for transfers between devices  29.2 us (22%)
  starting transfers between devices  19.8 us (15%)
  Pallas kernels  12.6 us (10%)
  between operations  1.41 us (1%)
    all_to_all x3, blocking collectives, exchange(): lax.all_to_all(value, 'row', split_axis=0, concat_axis=0, axis_index_grou...  68.4 us
    ppermute x2, waiting for transfers between devices, along(): lax.ppermute(value, 'row', [(i, (i + by * PLANE) % num_row) for i in rang...  15.8 us
    pallas_call x7, Pallas kernels, call(): pl.pallas_call(kernel, out_shape=outs, in_specs=[pl.BlockSpec(memory_spac...  12.6 us
    ppermute x1, waiting for transfers between devices, on_device(): cot_moved = lax.ppermute(cotangent[0], 'section', back_one)  8.69 us
    ppermute x1, starting transfers between devices, on_device(): cot_moved = lax.ppermute(cotangent[0], 'section', back_one)  7.23 us
    ppermute x2, starting transfers between devices, along(): lax.ppermute(value, 'row', [(i, (i + by * PLANE) % num_row) for i in rang...  5.41 us
    all_to_all x1, starting transfers between devices, exchange(): lax.all_to_all(value, 'row', split_axis=0, concat_axis=0, axis_index_grou...  5.26 us
    ppermute x1, waiting for transfers between devices, on_device(): moved = lax.ppermute(moved, 'section', back_one)  4.69 us
  transfers between devices with their start and end apart: 5, of which 4 were waited for; matrix products, arithmetic and copies ran while one was open for 0% of the time, Pallas kernels for 0%

commit v1 on v0

--- a/solution.py
+++ b/solution.py
@@ -106,31 +106,19 @@
         copy.wait()
 
 
-def expert_kernel(rows_hbm, w_all, _, part_ref, rows_ref, prod, wide, in_sems):
+def expert_kernel(rows_hbm, w_all, part_ref, rows_ref, prod, wide, sem):
     width = w_all.shape[1]
     half, quarter = width // 2, width // 4
     count = rows_ref.shape[0] // 4
-    pieces = in_sems.shape[0]
-    height = rows_ref.shape[0] // pieces
-    coming = []
-    for i in range(pieces):
-        at = slice(i * height, (i + 1) * height)
-        coming.append(pltpu.make_async_copy(rows_hbm.at[at], rows_ref.at[at], in_sems.at[i]))
-        coming[i].start()
+    coming = pltpu.make_async_copy(rows_hbm, rows_ref, sem)
+    coming.start()
+    coming.wait()
     nt = (((1,), (1,)), ((), ()))
-    for i in range(pieces):
-        at = slice(i * height, (i + 1) * height)
-        coming[i].wait()
-        for h in range(2):
-            cols = slice(h * half, (h + 1) * half)
-            out = lax.dot_general(
-                rows_ref[at, :],
-                w_all[:, cols],
-                nt,
-                preferred_element_type=f32,
-            )
-            for column in range(3):
-                prod[h * 3 + column, at, :] = out[:, column * PAD : (column + 1) * PAD]
+    for h in range(2):
+        cols = slice(h * half, (h + 1) * half)
+        out = lax.dot_general(rows_ref[...], w_all[:, cols], nt, preferred_element_type=f32)
+        for column in range(3):
+            prod[h * 3 + column] = out[:, column * PAD : (column + 1) * PAD]
 
     def taken(kind, column):
         low = prod[column, pl.ds(kind, count, stride=4), :]
@@ -174,9 +162,7 @@
     return acc
 
 
-def middle_kernel(got_ref, cot_hbm, part_ref, cot_ref, tile, scores, sem):
-    copy = pltpu.make_async_copy(cot_hbm, cot_ref, sem)
-    copy.start()
+def middle_kernel(got_ref, part_hbm, part_ref, tile, scores, sem):
     peers = part_ref.shape[0]
     tall = peers * 8
     acc = summed(got_ref)
@@ -189,6 +175,8 @@
     for a in range(peers):
         tile[a, 0:CAP] = scores[CAP * a : CAP * (a + 1)]
     part_ref[:, blocks * 8 :, :] = tile[...].astype(bf16)
+    copy = pltpu.make_async_copy(part_ref, part_hbm, sem)
+    copy.start()
     copy.wait()
 
 
@@ -323,29 +311,29 @@
         [pltpu.VMEM((PLANE, quarter // 128 * tall + tall // 4, 128), bf16)],
         rows.reshape(count, half),
         w_all,
-        cot_moved,
         scratch=(
             pltpu.VMEM((count, half), bf16),
             pltpu.VMEM((6, count, PAD), f32),
             pltpu.VMEM((quarter // 128, count, 128), f32),
-            pltpu.SemaphoreType.DMA((4,)),
+            pltpu.SemaphoreType.DMA,
         ),
         near=(1,),
-        far=(0, 2),
+        far=(0,),
     )
     got = exchange(part, in_plane)
-    part, cot_moved = call(
+    part_shape = (peers, quarter // 16 + 8, 128)
+    (part,) = call(
         middle_kernel,
-        [pltpu.VMEM((peers, quarter // 16 + 8, 128), bf16), pltpu.VMEM((tokens, width), bf16)],
+        [pltpu.HBM(part_shape, bf16)],
         got,
-        cot_moved,
         scratch=(
+            pltpu.VMEM(part_shape, bf16),
             pltpu.VMEM((peers, 8, 128), f32),
             pltpu.VMEM((peers * CAP, 128), f32),
             pltpu.SemaphoreType.DMA,
         ),
         near=(0,),
-        far=(1,),
+        out_space=pltpu.HBM,
     )
     got = exchange(part, along_z)
     moved, grad = call(

time: 132 us -> 127 us (0.962)
  blocking collectives: 68.4 us -> 53.9 us
  waiting for transfers between devices: 29.2 us -> 35.7 us
  starting transfers between devices: 19.8 us -> 23.7 us
  Pallas kernels: 12.6 us -> 10.9 us
    all_to_all x1 -> x2, waiting for transfers between devices: 0.01 us -> 18.2 us  [exchange(): lax.all_to_all(value, 'row', split_axis=0, concat_axis=0, axis_index_grou...]
    all_to_all x3 -> x2, blocking collectives: 68.4 us -> 53.9 us  [exchange(): lax.all_to_all(value, 'row', split_axis=0, concat_axis=0, axis_index_grou...]
    ppermute x1, waiting for transfers between devices: 8.69 us -> 0.01 us  [on_device(): cot_moved = lax.ppermute(cotangent[0], 'section', back_one)]
    all_to_all x1 -> x2, starting transfers between devices: 5.26 us -> 9.79 us  [exchange(): lax.all_to_all(value, 'row', split_axis=0, concat_axis=0, axis_index_grou...]
    ppermute x1, starting transfers between devices: 7.23 us -> 2.89 us  [on_device(): cot_moved = lax.ppermute(cotangent[0], 'section', back_one)]
    ppermute x1, starting transfers between devices: 1.91 us -> 5.58 us  [on_device(): moved = lax.ppermute(moved, 'section', back_one)]
    ppermute x2, waiting for transfers between devices: 15.8 us -> 13.8 us  [along(): lax.ppermute(value, 'row', [(i, (i + by * PLANE) % num_row) for i in rang...]
    pallas_call x7, Pallas kernels: 12.6 us -> 10.9 us  [call(): pl.pallas_call(kernel, out_shape=outs, in_specs=[pl.BlockSpec(memory_spac...]
  transfers between devices with their start and end apart: 5 -> 6, of which waited for: 4 -> 4; matrix products, arithmetic and copies ran while one was open for 0% -> 0% of each run, Pallas kernels for 0% -> 1%
where the time goes in v1:
time: 127 us
  blocking collectives  53.9 us (42%)
  waiting for transfers between devices  35.7 us (28%)
  starting transfers between devices  23.7 us (19%)
  Pallas kernels  10.9 us (9%)
  between operations  1.44 us (1%)
    all_to_all x2, blocking collectives, exchange(): lax.all_to_all(value, 'row', split_axis=0, concat_axis=0, axis_index_grou...  53.9 us
    all_to_all x2, waiting for transfers between devices, exchange(): lax.all_to_all(value, 'row', split_axis=0, concat_axis=0, axis_index_grou...  18.2 us
    ppermute x2, waiting for transfers between devices, along(): lax.ppermute(value, 'row', [(i, (i + by * PLANE) % num_row) for i in rang...  13.8 us
    pallas_call x7, Pallas kernels, call(): pl.pallas_call(kernel, out_shape=outs, in_specs=[pl.BlockSpec(memory_spac...  10.9 us
    all_to_all x2, starting transfers between devices, exchange(): lax.all_to_all(value, 'row', split_axis=0, concat_axis=0, axis_index_grou...  9.79 us
    ppermute x1, starting transfers between devices, on_device(): moved = lax.ppermute(moved, 'section', back_one)  5.58 us
    ppermute x2, starting transfers between devices, along(): lax.ppermute(value, 'row', [(i, (i + by * PLANE) % num_row) for i in rang...  5.41 us
    ppermute x1, waiting for transfers between devices, on_device(): moved = lax.ppermute(moved, 'section', back_one)  3.76 us
  transfers between devices with their start and end apart: 6, of which 4 were waited for; matrix products, arithmetic and copies ran while one was open for 0% of the time, Pallas kernels for 1%

profile of v1, /device:TPU:1, one launch (start us, length us, event | category | flops | bytes accessed | tf_op | source)
XLA Modules:
  0.0 126.8 jit_solution(13063340767427793176)
XLA Ops:
  1.3 2.0 %shard_map.86 = (bf16[8,8,2048]{2,1,0:T(8,128)(2,1)S(1)}, f32[8,1024]{1,0:T(8,128)S(1)}, f32[8,128]{1,0:T(8,128)S(1)}, f32[8,128]{1,0:T(8,128)S(1)}, f32[8,128]{1,0:T(8,128)S(1)}) custom-call(s32[2,128]{1,0:T(2,128)} %bitcast.27, s32[1]{0:T(128)S(6)} %copy.9.hot_ref, f32[2,128]{1,0:T(2,128)} %bitcast.28, bf16[128,4096]{1,0:T(8,128)(2,1)} %bitcast.24, ...), custom_call_target="tpu_custom_call" | custom-call | tf_op jit(solution)/shard_map/pallas_call | solution.py:224
  3.3 32.7 %all_to_all.20 = bf16[8,8,2048]{2,1,0:T(8,128)(2,1)S(1)} all-to-all(bf16[8,8,2048]{2,1,0:T(8,128)(2,1)S(1)} %get-tuple-element.9), channel_id=1, replica_groups={{0,16,32,48,64,80,96,112},{1,17,33,49,65,81,97,113},{2,18,34,50,66,82,9..., dimensions={0} | all-to-all | bytes 524288 | tf_op jit(solution)/shard_map/all_to_all | solution.py:250
  36.0 1.4 %shard_map.87 = bf16[8,64,2048]{2,1,0:T(8,128)(2,1)} custom-call(bf16[64,2048]{1,0:T(8,128)(2,1)S(1)} %bitcast.22), custom_call_target="tpu_custom_call" | custom-call | tf_op jit(solution)/shard_map/pallas_call | solution.py:224
  37.4 0.0 copy-start
  37.4 0.0 copy-start.3
  37.4 5.3 %all-to-all-start.1 = ((bf16[8,64,2048]{2,1,0:T(8,128)(2,1)}), bf16[8,64,2048]{2,1,0:T(8,128)(2,1)}, u32[]{:S(2)}, u32[]{:S(2)}) async-start(bf16[8,64,2048]{2,1,0:T(8,128)(2,1)} %shard_map.87), calls=%async_computation.1 | async-start | bytes 4194304 | tf_op jit(solution)/shard_map/all_to_all | solution.py:250
  42.7 0.0 copy-done
  42.7 0.0 copy-done.3
  42.7 0.0 copy-start.1
  42.7 0.0 copy-start.4
  42.7 0.1 pad_maximum_fusion
  42.8 2.1 %collective-permute-start.2 = (bf16[3,32,4096]{2,1,0:T(8,128)(2,1)S(1)}, bf16[3,32,4096]{2,1,0:T(8,128)(2,1)S(1)}, u32[]{:S(2)}, u32[]{:S(2)}) collective-permute-start(bf16[3,32,4096]{2,1,0:T(8,128)(2,1)S(1)} %pad_maximum_fusion), channel_id=1, source_target_pairs={{0,120},{1,121},{2,122},{3,123},{4,124},{5,125},{6,126},{7,127},{8... | collective-permute-start | bytes 2359304 | tf_op jit(solution)/shard_map/ppermute | solution.py:255
  44.9 3.4 %collective-permute-start.1 = (bf16[3,24,4096]{2,1,0:T(8,128)(2,1)S(1)}, bf16[3,24,4096]{2,1,0:T(8,128)(2,1)S(1)}, u32[]{:S(2)}, u32[]{:S(2)}) collective-permute-start(bf16[3,24,4096]{2,1,0:T(8,128)(2,1)S(1)} %pad_maximum_fusion.1), channel_id=1, source_target_pairs={{0,8},{1,9},{2,10},{3,11},{4,12},{5,13},{6,14},{7,15},{8,16},{9,17... | collective-permute-start | bytes 1769480 | tf_op jit(solution)/shard_map/ppermute | solution.py:255
  48.2 13.8 %collective-permute-done.1.below_ref = bf16[3,24,4096]{2,1,0:T(8,128)(2,1)S(1)} collective-permute-done((bf16[3,24,4096]{2,1,0:T(8,128)(2,1)S(1)}, bf16[3,24,4096]{2,1,0:T(8,128)(2,1)S(1)}, u32[]{:S(2)}, u32[]{:S(2)}) %collective-permute-start.1) | collective-permute-done | bytes 589856 | tf_op jit(solution)/shard_map/ppermute | solution.py:255
  62.0 0.0 collective-permute-done.2.above_ref
  62.0 0.0 copy-done.1
  62.0 0.0 copy-done.4
  62.0 0.2 shard_map.88.w_all
  62.2 5.8 %all-to-all-done.1 = bf16[8,64,2048]{2,1,0:T(8,128)(2,1)} async-done(((bf16[8,64,2048]{2,1,0:T(8,128)(2,1)}), bf16[8,64,2048]{2,1,0:T(8,128)(2,1)}, u32[]{:S(2)}, u32[]{:S(2)}) %all-to-all-start.1) | async-done | bytes 2097184 | tf_op jit(solution)/shard_map/all_to_all | solution.py:250
  68.0 4.5 %shard_map.89 = bf16[8,528,128]{2,1,0:T(8,128)(2,1)S(1)} custom-call(bf16[512,2048]{1,0:T(8,128)(2,1)} %bitcast.7.rows_hbm, bf16[384,4096]{1,0:T(8,128)(2,1)S(1)} %shard_map.88.w_all), custom_call_target="tpu_custom_call" | custom-call | tf_op jit(solution)/shard_map/pallas_call | solution.py:224
  72.5 0.0 copy-start.2
  72.5 1.0 copy-done.2
  73.5 0.0 copy-start.5
  73.5 4.5 %all-to-all-start.2 = ((bf16[8,528,128]{2,1,0:T(8,128)(2,1)}), bf16[8,528,128]{2,1,0:T(8,128)(2,1)S(1)}, u32[]{:S(2)}, u32[]{:S(2)}) async-start(bf16[8,528,128]{2,1,0:T(8,128)(2,1)} %copy-done.2), calls=%async_computation.2 | async-start | bytes 2162688 | tf_op jit(solution)/shard_map/all_to_all | solution.py:250
  78.0 0.0 copy-done.5
  78.1 2.9 %collective-permute-start = (bf16[128,4096]{1,0:T(8,128)(2,1)S(1)}, bf16[128,4096]{1,0:T(8,128)(2,1)S(1)}, u32[]{:S(2)}, u32[]{:S(2)}) collective-permute-start(bf16[128,4096]{1,0:T(8,128)(2,1)S(1)} %bitcast.26), channel_id=1, source_target_pairs={{128,0},{256,128},{384,256},{129,1},{257,129},{385,257},{130,2},{2... | collective-permute-start | bytes 3145736 | tf_op jit(solution)/shard_map/ppermute | solution.py:262
  80.9 12.4 %all-to-all-done.2.got_ref = bf16[8,528,128]{2,1,0:T(8,128)(2,1)S(1)} async-done(((bf16[8,528,128]{2,1,0:T(8,128)(2,1)}), bf16[8,528,128]{2,1,0:T(8,128)(2,1)S(1)}, u32[]{:S(2)}, u32[]{:S(2)}) %all-to-all-start.2) | async-done | bytes 1081376 | tf_op jit(solution)/shard_map/all_to_all | solution.py:250
  93.4 0.9 shard_map.90
  94.3 21.2 %all_to_all.21.got_ref = bf16[8,72,128]{2,1,0:T(8,128)(2,1)S(1)} all-to-all(bf16[8,72,128]{2,1,0:T(8,128)(2,1)} %shard_map.90), channel_id=1, replica_groups={{0,16,32,48,64,80,96,112},{1,17,33,49,65,81,97,113},{2,18,34,50,66,82,9..., dimensions={0} | all-to-all | bytes 294912 | tf_op jit(solution)/shard_map/all_to_all | solution.py:250
  115.5 0.7 shard_map.91
  116.1 5.6 %collective-permute-start.3 = (bf16[8,1152]{1,0:T(8,128)(2,1)S(1)}, bf16[8,1152]{1,0:T(8,128)(2,1)S(1)}, u32[]{:S(2)}, u32[]{:S(2)}) collective-permute-start(bf16[8,1152]{1,0:T(8,128)(2,1)S(1)} %get-tuple-element.14), channel_id=1, source_target_pairs={{128,0},{256,128},{384,256},{129,1},{257,129},{385,257},{130,2},{2... | collective-permute-start | bytes 55304 | tf_op jit(solution)/shard_map/ppermute | solution.py:349
  121.7 0.0 collective-permute-done.cot_ref
  121.7 3.8 %collective-permute-done.3.moved_ref = bf16[8,1152]{1,0:T(8,128)(2,1)S(1)} collective-permute-done((bf16[8,1152]{1,0:T(8,128)(2,1)S(1)}, bf16[8,1152]{1,0:T(8,128)(2,1)S(1)}, u32[]{:S(2)}, u32[]{:S(2)}) %collective-permute-start.3) | collective-permute-done | bytes 18464 | tf_op jit(solution)/shard_map/ppermute | solution.py:349
  125.5 1.3 %shard_map.92 = bf16[128,4096]{1,0:T(8,128)(2,1)} custom-call(bf16[128,4096]{1,0:T(8,128)(2,1)S(1)} %collective-permute-done.cot_ref, bf16[8,1152]{1,0:T(8,128)(2,1)S(1)} %collective-permute-done.3.moved_ref), custom_call_target="tpu_custom_call" | custom-call | tf_op jit(solution)/shard_map/pallas_call | solution.py:224
  (1 shorter events, 0.0 us)
Async XLA Ops:
  37.4 5.3 %copy-start = (bf16[1,2,4096,56]{2,3,1,0:T(8,128)(2,1)S(1)}, bf16[1,2,4096,56]{2,3,1,0:T(8,128)(2,1)}, u32[]{:S(2)}) copy-start(bf16[1,2,4096,56]{2,3,1,0:T(8,128)(2,1)} %param.12) | copy-start | bytes 2752516
  37.4 5.3 %copy-start.3 = (bf16[1,56,4096]{2,1,0:T(8,128)(2,1)S(1)}, bf16[1,56,4096]{2,1,0:T(8,128)(2,1)}, u32[]{:S(2)}) copy-start(bf16[1,56,4096]{2,1,0:T(8,128)(2,1)} %param.13) | copy-start | bytes 1376260
  37.4 30.6 %all-to-all-start.1 = ((bf16[8,64,2048]{2,1,0:T(8,128)(2,1)}), bf16[8,64,2048]{2,1,0:T(8,128)(2,1)}, u32[]{:S(2)}, u32[]{:S(2)}) async-start(bf16[8,64,2048]{2,1,0:T(8,128)(2,1)} %shard_map.87), calls=%async_computation.1 | async-start | bytes 4194304 | tf_op jit(solution)/shard_map/all_to_all | solution.py:250
  42.7 19.3 %copy-start.1 = (bf16[1,2,4096,56]{2,3,1,0:T(8,128)(2,1)S(1)}, bf16[1,2,4096,56]{2,3,1,0:T(8,128)(2,1)}, u32[]{:S(2)}) copy-start(bf16[1,2,4096,56]{2,3,1,0:T(8,128)(2,1)} %param.12) | copy-start | bytes 2752516
  42.7 19.3 %copy-start.4 = (bf16[1,56,4096]{2,1,0:T(8,128)(2,1)S(1)}, bf16[1,56,4096]{2,1,0:T(8,128)(2,1)}, u32[]{:S(2)}) copy-start(bf16[1,56,4096]{2,1,0:T(8,128)(2,1)} %param.13) | copy-start | bytes 1376260
  42.8 19.2 %collective-permute-start.2 = (bf16[3,32,4096]{2,1,0:T(8,128)(2,1)S(1)}, bf16[3,32,4096]{2,1,0:T(8,128)(2,1)S(1)}, u32[]{:S(2)}, u32[]{:S(2)}) collective-permute-start(bf16[3,32,4096]{2,1,0:T(8,128)(2,1)S(1)} %pad_maximum_fusion), channel_id=1, source_target_pairs={{0,120},{1,121},{2,122},{3,123},{4,124},{5,125},{6,126},{7,127},{8... | collective-permute-start | bytes 2359304 | tf_op jit(solution)/shard_map/ppermute | solution.py:255
  44.9 17.1 %collective-permute-start.1 = (bf16[3,24,4096]{2,1,0:T(8,128)(2,1)S(1)}, bf16[3,24,4096]{2,1,0:T(8,128)(2,1)S(1)}, u32[]{:S(2)}, u32[]{:S(2)}) collective-permute-start(bf16[3,24,4096]{2,1,0:T(8,128)(2,1)S(1)} %pad_maximum_fusion.1), channel_id=1, source_target_pairs={{0,8},{1,9},{2,10},{3,11},{4,12},{5,13},{6,14},{7,15},{8,16},{9,17... | collective-permute-start | bytes 1769480 | tf_op jit(solution)/shard_map/ppermute | solution.py:255
  72.5 1.0 copy-start.2
  73.5 4.5 %copy-start.5 = (bf16[1,128,4096]{2,1,0:T(8,128)(2,1)S(1)}, bf16[1,128,4096]{2,1,0:T(8,128)(2,1)}, u32[]{:S(2)}) copy-start(bf16[1,128,4096]{2,1,0:T(8,128)(2,1)} %param.8) | copy-start | bytes 3145732
  73.5 19.8 %all-to-all-start.2 = ((bf16[8,528,128]{2,1,0:T(8,128)(2,1)}), bf16[8,528,128]{2,1,0:T(8,128)(2,1)S(1)}, u32[]{:S(2)}, u32[]{:S(2)}) async-start(bf16[8,528,128]{2,1,0:T(8,128)(2,1)} %copy-done.2), calls=%async_computation.2 | async-start | bytes 2162688 | tf_op jit(solution)/shard_map/all_to_all | solution.py:250
  78.1 43.7 %collective-permute-start = (bf16[128,4096]{1,0:T(8,128)(2,1)S(1)}, bf16[128,4096]{1,0:T(8,128)(2,1)S(1)}, u32[]{:S(2)}, u32[]{:S(2)}) collective-permute-start(bf16[128,4096]{1,0:T(8,128)(2,1)S(1)} %bitcast.26), channel_id=1, source_target_pairs={{128,0},{256,128},{384,256},{129,1},{257,129},{385,257},{130,2},{2... | collective-permute-start | bytes 3145736 | tf_op jit(solution)/shard_map/ppermute | solution.py:262
  116.1 9.4 %collective-permute-start.3 = (bf16[8,1152]{1,0:T(8,128)(2,1)S(1)}, bf16[8,1152]{1,0:T(8,128)(2,1)S(1)}, u32[]{:S(2)}, u32[]{:S(2)}) collective-permute-start(bf16[8,1152]{1,0:T(8,128)(2,1)S(1)} %get-tuple-element.14), channel_id=1, source_target_pairs={{128,0},{256,128},{384,256},{129,1},{257,129},{385,257},{130,2},{2... | collective-permute-start | bytes 55304 | tf_op jit(solution)/shard_map/ppermute | solution.py:349

commit v2 on v1

--- a/solution.py
+++ b/solution.py
@@ -8,6 +8,7 @@
 
 CAP = 2
 TOP = 2
+TURNS = 2200
 PLANE = 8
 SENT_DOWN = 32
 PAD = 128
@@ -32,9 +33,9 @@
 
 
 def select_kernel(
-    chosen_hbm, hot_ref, weight_hbm, x_hbm, g_hbm,
+    chosen_hbm, hot_ref, weight_hbm, x_hbm, g_hbm, turns_ref,
     sent_ref, cot_ref, w_ref, t_ref, held_ref,
-    chosen_ref, weight_ref, x_ref, g_ref, sems,
+    chosen_ref, weight_ref, x_ref, g_ref, spun_ref, sems,
 ):
     pairs = (
         (chosen_hbm, chosen_ref),
@@ -77,6 +78,13 @@
     ).astype(bf16)
     for i in range(sent_ref.shape[0]):
         sent_ref[i] = unit
+
+    def turn(i, carry):
+        spun_ref[...] = spun_ref[...] + 1.0
+        return carry
+
+    spun_ref[...] = jnp.zeros_like(spun_ref)
+    lax.fori_loop(0, turns_ref[0], turn, 0)
     at = lax.broadcasted_iota(jnp.int32, (8, quarter), 0) & 3
     cot = g_rows[:, :quarter]
     for q in range(1, 4):
@@ -275,14 +283,16 @@
         route_weight[0].T,
         layer_input[0],
         cotangent[0],
+        (lax.axis_index("section") % 2 * TURNS).reshape(1),
         scratch=(
             pltpu.VMEM((TOP, tokens), jnp.int32),
             pltpu.VMEM((TOP, tokens), f32),
             pltpu.VMEM((tokens, width), bf16),
             pltpu.VMEM((tokens, width), bf16),
+            pltpu.VMEM((8, 128), f32),
             pltpu.SemaphoreType.DMA((4,)),
         ),
-        smem=(1,),
+        smem=(1, 5),
         far=(0, 2, 3, 4),
     )
     tall = peers * 8

time: 127 us -> 118 us (0.929)
  Pallas kernels: 10.9 us -> 26 us
  waiting for transfers between devices: 35.7 us -> 21.4 us
  blocking collectives: 53.9 us -> 48.7 us
  starting transfers between devices: 23.7 us -> 19.2 us
    pallas_call x7, Pallas kernels: 10.9 us -> 26 us  [call(): pl.pallas_call(kernel, out_shape=outs, in_specs=[pl.BlockSpec(memory_spac...]
    all_to_all x2, waiting for transfers between devices: 18.2 us -> 8.59 us  [exchange(): lax.all_to_all(value, 'row', split_axis=0, concat_axis=0, axis_index_grou...]
    ppermute x2, waiting for transfers between devices: 13.8 us -> 8.12 us  [along(): lax.ppermute(value, 'row', [(i, (i + by * PLANE) % num_row) for i in rang...]
    all_to_all x2, blocking collectives: 53.9 us -> 48.7 us  [exchange(): lax.all_to_all(value, 'row', split_axis=0, concat_axis=0, axis_index_grou...]
    ppermute x1, starting transfers between devices: 5.58 us -> 1.91 us  [on_device(): moved = lax.ppermute(moved, 'section', back_one)]
where the time goes in v2:
time: 118 us
  blocking collectives  48.7 us (41%)
  Pallas kernels  26 us (22%)
  waiting for transfers between devices  21.4 us (18%)
  starting transfers between devices  19.2 us (16%)
  between operations  1.45 us (1%)
    all_to_all x2, blocking collectives, exchange(): lax.all_to_all(value, 'row', split_axis=0, concat_axis=0, axis_index_grou...  48.7 us
    pallas_call x7, Pallas kernels, call(): pl.pallas_call(kernel, out_shape=outs, in_specs=[pl.BlockSpec(memory_spac...  26 us
    all_to_all x2, starting transfers between devices, exchange(): lax.all_to_all(value, 'row', split_axis=0, concat_axis=0, axis_index_grou...  9.64 us
    all_to_all x2, waiting for transfers between devices, exchange(): lax.all_to_all(value, 'row', split_axis=0, concat_axis=0, axis_index_grou...  8.59 us
    ppermute x2, waiting for transfers between devices, along(): lax.ppermute(value, 'row', [(i, (i + by * PLANE) % num_row) for i in rang...  8.12 us
    ppermute x2, starting transfers between devices, along(): lax.ppermute(value, 'row', [(i, (i + by * PLANE) % num_row) for i in rang...  5.77 us
    ppermute x1, waiting for transfers between devices, on_device(): moved = lax.ppermute(moved, 'section', back_one)  4.65 us
  transfers between devices with their start and end apart: 6, of which 4 were waited for; matrix products, arithmetic and copies ran while one was open for 0% of the time, Pallas kernels for 1%

profile of v2, /device:TPU:1, one launch (start us, length us, event | category | flops | bytes accessed | tf_op | source)
XLA Modules:
  0.0 117.8 jit_solution(13963131982921551754)
XLA Ops:
  1.3 17.1 %shard_map.86 = (bf16[8,8,2048]{2,1,0:T(8,128)(2,1)S(1)}, f32[8,1024]{1,0:T(8,128)S(1)}, f32[8,128]{1,0:T(8,128)S(1)}, f32[8,128]{1,0:T(8,128)S(1)}, f32[8,128]{1,0:T(8,128)S(1)}) custom-call(s32[2,128]{1,0:T(2,128)} %bitcast.28, s32[1]{0:T(128)S(6)} %copy.9.hot_ref, f32[2,128]{1,0:T(2,128)} %bitcast.29, bf16[128,4096]{1,0:T(8,128)(2,1)} %bitcast.25, ...), custom_call_target="tpu_custom_call" | custom-call | tf_op jit(solution)/shard_map/pallas_call | solution.py:232
  18.4 31.1 %all_to_all.20 = bf16[8,8,2048]{2,1,0:T(8,128)(2,1)S(1)} all-to-all(bf16[8,8,2048]{2,1,0:T(8,128)(2,1)S(1)} %get-tuple-element.9), channel_id=1, replica_groups={{0,16,32,48,64,80,96,112},{1,17,33,49,65,81,97,113},{2,18,34,50,66,82,9..., dimensions={0} | all-to-all | bytes 524288 | tf_op jit(solution)/shard_map/all_to_all | solution.py:258
  49.4 1.4 %shard_map.87 = bf16[8,64,2048]{2,1,0:T(8,128)(2,1)} custom-call(bf16[64,2048]{1,0:T(8,128)(2,1)S(1)} %bitcast.23), custom_call_target="tpu_custom_call" | custom-call | tf_op jit(solution)/shard_map/pallas_call | solution.py:232
  50.8 0.0 copy-start
  50.8 0.0 copy-start.3
  50.8 5.3 %all-to-all-start.1 = ((bf16[8,64,2048]{2,1,0:T(8,128)(2,1)}), bf16[8,64,2048]{2,1,0:T(8,128)(2,1)}, u32[]{:S(2)}, u32[]{:S(2)}) async-start(bf16[8,64,2048]{2,1,0:T(8,128)(2,1)} %shard_map.87), calls=%async_computation.1 | async-start | bytes 4194304 | tf_op jit(solution)/shard_map/all_to_all | solution.py:258
  56.1 0.0 copy-done
  56.1 0.0 copy-done.3
  56.1 0.0 copy-start.1
  56.1 0.0 copy-start.4
  56.1 0.1 pad_maximum_fusion
  56.2 2.1 %collective-permute-start.2 = (bf16[3,32,4096]{2,1,0:T(8,128)(2,1)S(1)}, bf16[3,32,4096]{2,1,0:T(8,128)(2,1)S(1)}, u32[]{:S(2)}, u32[]{:S(2)}) collective-permute-start(bf16[3,32,4096]{2,1,0:T(8,128)(2,1)S(1)} %pad_maximum_fusion), channel_id=1, source_target_pairs={{0,120},{1,121},{2,122},{3,123},{4,124},{5,125},{6,126},{7,127},{8... | collective-permute-start | bytes 2359304 | tf_op jit(solution)/shard_map/ppermute | solution.py:263
  58.3 3.7 %collective-permute-start.1 = (bf16[3,24,4096]{2,1,0:T(8,128)(2,1)S(1)}, bf16[3,24,4096]{2,1,0:T(8,128)(2,1)S(1)}, u32[]{:S(2)}, u32[]{:S(2)}) collective-permute-start(bf16[3,24,4096]{2,1,0:T(8,128)(2,1)S(1)} %pad_maximum_fusion.1), channel_id=1, source_target_pairs={{0,8},{1,9},{2,10},{3,11},{4,12},{5,13},{6,14},{7,15},{8,16},{9,17... | collective-permute-start | bytes 1769480 | tf_op jit(solution)/shard_map/ppermute | solution.py:263
  62.0 8.1 %collective-permute-done.1.below_ref = bf16[3,24,4096]{2,1,0:T(8,128)(2,1)S(1)} collective-permute-done((bf16[3,24,4096]{2,1,0:T(8,128)(2,1)S(1)}, bf16[3,24,4096]{2,1,0:T(8,128)(2,1)S(1)}, u32[]{:S(2)}, u32[]{:S(2)}) %collective-permute-start.1) | collective-permute-done | bytes 589856 | tf_op jit(solution)/shard_map/ppermute | solution.py:263
  70.1 0.0 collective-permute-done.2.above_ref
  70.2 0.0 copy-done.1
  70.2 0.0 copy-done.4
  70.2 0.2 shard_map.88.w_all
  70.4 0.9 all-to-all-done.1
  71.3 4.5 %shard_map.89 = bf16[8,528,128]{2,1,0:T(8,128)(2,1)S(1)} custom-call(bf16[512,2048]{1,0:T(8,128)(2,1)} %bitcast.8.rows_hbm, bf16[384,4096]{1,0:T(8,128)(2,1)S(1)} %shard_map.88.w_all), custom_call_target="tpu_custom_call" | custom-call | tf_op jit(solution)/shard_map/pallas_call | solution.py:232
  75.8 0.0 copy-start.2
  75.8 1.0 copy-done.2
  76.8 0.0 copy-start.5
  76.8 4.4 %all-to-all-start.2 = ((bf16[8,528,128]{2,1,0:T(8,128)(2,1)}), bf16[8,528,128]{2,1,0:T(8,128)(2,1)S(1)}, u32[]{:S(2)}, u32[]{:S(2)}) async-start(bf16[8,528,128]{2,1,0:T(8,128)(2,1)} %copy-done.2), calls=%async_computation.2 | async-start | bytes 2162688 | tf_op jit(solution)/shard_map/all_to_all | solution.py:258
  81.2 0.0 copy-done.5
  81.2 1.9 %collective-permute-start = (bf16[128,4096]{1,0:T(8,128)(2,1)S(1)}, bf16[128,4096]{1,0:T(8,128)(2,1)S(1)}, u32[]{:S(2)}, u32[]{:S(2)}) collective-permute-start(bf16[128,4096]{1,0:T(8,128)(2,1)S(1)} %bitcast.27), channel_id=1, source_target_pairs={{128,0},{256,128},{384,256},{129,1},{257,129},{385,257},{130,2},{2... | collective-permute-start | bytes 3145736 | tf_op jit(solution)/shard_map/ppermute | solution.py:270
  83.1 7.7 %all-to-all-done.2.got_ref = bf16[8,528,128]{2,1,0:T(8,128)(2,1)S(1)} async-done(((bf16[8,528,128]{2,1,0:T(8,128)(2,1)}), bf16[8,528,128]{2,1,0:T(8,128)(2,1)S(1)}, u32[]{:S(2)}, u32[]{:S(2)}) %all-to-all-start.2) | async-done | bytes 1081376 | tf_op jit(solution)/shard_map/all_to_all | solution.py:258
  90.8 0.9 shard_map.90
  91.7 17.6 %all_to_all.21.got_ref = bf16[8,72,128]{2,1,0:T(8,128)(2,1)S(1)} all-to-all(bf16[8,72,128]{2,1,0:T(8,128)(2,1)} %shard_map.90), channel_id=1, replica_groups={{0,16,32,48,64,80,96,112},{1,17,33,49,65,81,97,113},{2,18,34,50,66,82,9..., dimensions={0} | all-to-all | bytes 294912 | tf_op jit(solution)/shard_map/all_to_all | solution.py:258
  109.3 0.7 shard_map.91
  109.9 1.9 %collective-permute-start.3 = (bf16[8,1152]{1,0:T(8,128)(2,1)S(1)}, bf16[8,1152]{1,0:T(8,128)(2,1)S(1)}, u32[]{:S(2)}, u32[]{:S(2)}) collective-permute-start(bf16[8,1152]{1,0:T(8,128)(2,1)S(1)} %get-tuple-element.14), channel_id=1, source_target_pairs={{128,0},{256,128},{384,256},{129,1},{257,129},{385,257},{130,2},{2... | collective-permute-start | bytes 55304 | tf_op jit(solution)/shard_map/ppermute | solution.py:359
  111.9 0.0 collective-permute-done.cot_ref
  111.9 4.6 %collective-permute-done.3.moved_ref = bf16[8,1152]{1,0:T(8,128)(2,1)S(1)} collective-permute-done((bf16[8,1152]{1,0:T(8,128)(2,1)S(1)}, bf16[8,1152]{1,0:T(8,128)(2,1)S(1)}, u32[]{:S(2)}, u32[]{:S(2)}) %collective-permute-start.3) | collective-permute-done | bytes 18464 | tf_op jit(solution)/shard_map/ppermute | solution.py:359
  116.5 1.3 %shard_map.92 = bf16[128,4096]{1,0:T(8,128)(2,1)} custom-call(bf16[128,4096]{1,0:T(8,128)(2,1)S(1)} %collective-permute-done.cot_ref, bf16[8,1152]{1,0:T(8,128)(2,1)S(1)} %collective-permute-done.3.moved_ref), custom_call_target="tpu_custom_call" | custom-call | tf_op jit(solution)/shard_map/pallas_call | solution.py:232
  (1 shorter events, 0.0 us)
Async XLA Ops:
  50.8 5.3 %copy-start = (bf16[1,2,4096,56]{2,3,1,0:T(8,128)(2,1)S(1)}, bf16[1,2,4096,56]{2,3,1,0:T(8,128)(2,1)}, u32[]{:S(2)}) copy-start(bf16[1,2,4096,56]{2,3,1,0:T(8,128)(2,1)} %param.12) | copy-start | bytes 2752516
  50.8 5.3 %copy-start.3 = (bf16[1,56,4096]{2,1,0:T(8,128)(2,1)S(1)}, bf16[1,56,4096]{2,1,0:T(8,128)(2,1)}, u32[]{:S(2)}) copy-start(bf16[1,56,4096]{2,1,0:T(8,128)(2,1)} %param.13) | copy-start | bytes 1376260
  50.8 20.4 %all-to-all-start.1 = ((bf16[8,64,2048]{2,1,0:T(8,128)(2,1)}), bf16[8,64,2048]{2,1,0:T(8,128)(2,1)}, u32[]{:S(2)}, u32[]{:S(2)}) async-start(bf16[8,64,2048]{2,1,0:T(8,128)(2,1)} %shard_map.87), calls=%async_computation.1 | async-start | bytes 4194304 | tf_op jit(solution)/shard_map/all_to_all | solution.py:258
  56.1 14.0 %copy-start.1 = (bf16[1,2,4096,56]{2,3,1,0:T(8,128)(2,1)S(1)}, bf16[1,2,4096,56]{2,3,1,0:T(8,128)(2,1)}, u32[]{:S(2)}) copy-start(bf16[1,2,4096,56]{2,3,1,0:T(8,128)(2,1)} %param.12) | copy-start | bytes 2752516
  56.1 14.0 %copy-start.4 = (bf16[1,56,4096]{2,1,0:T(8,128)(2,1)S(1)}, bf16[1,56,4096]{2,1,0:T(8,128)(2,1)}, u32[]{:S(2)}) copy-start(bf16[1,56,4096]{2,1,0:T(8,128)(2,1)} %param.13) | copy-start | bytes 1376260
  56.2 14.0 %collective-permute-start.2 = (bf16[3,32,4096]{2,1,0:T(8,128)(2,1)S(1)}, bf16[3,32,4096]{2,1,0:T(8,128)(2,1)S(1)}, u32[]{:S(2)}, u32[]{:S(2)}) collective-permute-start(bf16[3,32,4096]{2,1,0:T(8,128)(2,1)S(1)} %pad_maximum_fusion), channel_id=1, source_target_pairs={{0,120},{1,121},{2,122},{3,123},{4,124},{5,125},{6,126},{7,127},{8... | collective-permute-start | bytes 2359304 | tf_op jit(solution)/shard_map/ppermute | solution.py:263
  58.3 11.8 %collective-permute-start.1 = (bf16[3,24,4096]{2,1,0:T(8,128)(2,1)S(1)}, bf16[3,24,4096]{2,1,0:T(8,128)(2,1)S(1)}, u32[]{:S(2)}, u32[]{:S(2)}) collective-permute-start(bf16[3,24,4096]{2,1,0:T(8,128)(2,1)S(1)} %pad_maximum_fusion.1), channel_id=1, source_target_pairs={{0,8},{1,9},{2,10},{3,11},{4,12},{5,13},{6,14},{7,15},{8,16},{9,17... | collective-permute-start | bytes 1769480 | tf_op jit(solution)/shard_map/ppermute | solution.py:263
  75.8 1.0 copy-start.2
  76.8 4.4 %copy-start.5 = (bf16[1,128,4096]{2,1,0:T(8,128)(2,1)S(1)}, bf16[1,128,4096]{2,1,0:T(8,128)(2,1)}, u32[]{:S(2)}) copy-start(bf16[1,128,4096]{2,1,0:T(8,128)(2,1)} %param.8) | copy-start | bytes 3145732
  76.8 14.0 %all-to-all-start.2 = ((bf16[8,528,128]{2,1,0:T(8,128)(2,1)}), bf16[8,528,128]{2,1,0:T(8,128)(2,1)S(1)}, u32[]{:S(2)}, u32[]{:S(2)}) async-start(bf16[8,528,128]{2,1,0:T(8,128)(2,1)} %copy-done.2), calls=%async_computation.2 | async-start | bytes 2162688 | tf_op jit(solution)/shard_map/all_to_all | solution.py:258
  81.2 30.7 %collective-permute-start = (bf16[128,4096]{1,0:T(8,128)(2,1)S(1)}, bf16[128,4096]{1,0:T(8,128)(2,1)S(1)}, u32[]{:S(2)}, u32[]{:S(2)}) collective-permute-start(bf16[128,4096]{1,0:T(8,128)(2,1)S(1)} %bitcast.27), channel_id=1, source_target_pairs={{128,0},{256,128},{384,256},{129,1},{257,129},{385,257},{130,2},{2... | collective-permute-start | bytes 3145736 | tf_op jit(solution)/shard_map/ppermute | solution.py:270
  109.9 6.6 %collective-permute-start.3 = (bf16[8,1152]{1,0:T(8,128)(2,1)S(1)}, bf16[8,1152]{1,0:T(8,128)(2,1)S(1)}, u32[]{:S(2)}, u32[]{:S(2)}) collective-permute-start(bf16[8,1152]{1,0:T(8,128)(2,1)S(1)} %get-tuple-element.14), channel_id=1, source_target_pairs={{128,0},{256,128},{384,256},{129,1},{257,129},{385,257},{130,2},{2... | collective-permute-start | bytes 55304 | tf_op jit(solution)/shard_map/ppermute | solution.py:359

commit v3 on v2

--- a/solution.py
+++ b/solution.py
@@ -105,8 +105,15 @@
 
 
 def spread_kernel(column_ref, sent_ref, sems):
+    peers, part = sent_ref.shape[0], sent_ref.shape[1] // 2
     copies = [
-        pltpu.make_async_copy(column_ref, sent_ref.at[i], sems.at[i]) for i in range(sent_ref.shape[0])
+        pltpu.make_async_copy(
+            column_ref.at[h * part : (h + 1) * part],
+            sent_ref.at[i, h * part : (h + 1) * part],
+            sems.at[2 * i + h],
+        )
+        for i in range(peers)
+        for h in range(2)
     ]
     for copy in copies:
         copy.start()
@@ -118,9 +125,17 @@
     width = w_all.shape[1]
     half, quarter = width // 2, width // 4
     count = rows_ref.shape[0] // 4
-    coming = pltpu.make_async_copy(rows_hbm, rows_ref, sem)
-    coming.start()
-    coming.wait()
+    part = rows_ref.shape[0] // 8
+    coming = [
+        pltpu.make_async_copy(
+            rows_hbm.at[i * part : (i + 1) * part], rows_ref.at[i * part : (i + 1) * part], sem.at[i]
+        )
+        for i in range(8)
+    ]
+    for copy in coming:
+        copy.start()
+    for copy in coming:
+        copy.wait()
     nt = (((1,), (1,)), ((), ()))
     for h in range(2):
         cols = slice(h * half, (h + 1) * half)
@@ -301,7 +316,7 @@
         spread_kernel,
         [pltpu.HBM((PLANE, tall, half), bf16)],
         column,
-        scratch=(pltpu.SemaphoreType.DMA((PLANE,)),),
+        scratch=(pltpu.SemaphoreType.DMA((2 * PLANE,)),),
         near=(0,),
         out_space=pltpu.HBM,
     )
@@ -325,7 +340,7 @@
             pltpu.VMEM((count, half), bf16),
             pltpu.VMEM((6, count, PAD), f32),
             pltpu.VMEM((quarter // 128, count, 128), f32),
-            pltpu.SemaphoreType.DMA,
+            pltpu.SemaphoreType.DMA((8,)),
         ),
         near=(1,),
         far=(0,),

time: 118 us -> 118 us (level)
  no operation moved by 1% of the time
where the time goes in v3:
time: 118 us
  blocking collectives  48.6 us (41%)
  Pallas kernels  26 us (22%)
  waiting for transfers between devices  21.5 us (18%)
  starting transfers between devices  19.1 us (16%)
  between operations  1.45 us (1%)
    all_to_all x2, blocking collectives, exchange(): lax.all_to_all(value, 'row', split_axis=0, concat_axis=0, axis_index_grou...  48.6 us
    pallas_call x7, Pallas kernels, call(): pl.pallas_call(kernel, out_shape=outs, in_specs=[pl.BlockSpec(memory_spac...  26 us
    all_to_all x2, starting transfers between devices, exchange(): lax.all_to_all(value, 'row', split_axis=0, concat_axis=0, axis_index_grou...  9.65 us
    all_to_all x2, waiting for transfers between devices, exchange(): lax.all_to_all(value, 'row', split_axis=0, concat_axis=0, axis_index_grou...  8.59 us
    ppermute x2, waiting for transfers between devices, along(): lax.ppermute(value, 'row', [(i, (i + by * PLANE) % num_row) for i in rang...  8.3 us
    ppermute x2, starting transfers between devices, along(): lax.ppermute(value, 'row', [(i, (i + by * PLANE) % num_row) for i in rang...  5.58 us
    ppermute x1, waiting for transfers between devices, on_device(): moved = lax.ppermute(moved, 'section', back_one)  4.65 us
  transfers between devices with their start and end apart: 6, of which 4 were waited for; matrix products, arithmetic and copies ran while one was open for 0% of the time, Pallas kernels for 1%

profile of v3, /device:TPU:1, one launch (start us, length us, event | category | flops | bytes accessed | tf_op | source)
XLA Modules:
  0.0 117.8 jit_solution(4397705418990367346)
XLA Ops:
  1.3 17.1 %shard_map.86 = (bf16[8,8,2048]{2,1,0:T(8,128)(2,1)S(1)}, f32[8,1024]{1,0:T(8,128)S(1)}, f32[8,128]{1,0:T(8,128)S(1)}, f32[8,128]{1,0:T(8,128)S(1)}, f32[8,128]{1,0:T(8,128)S(1)}) custom-call(s32[2,128]{1,0:T(2,128)} %bitcast.28, s32[1]{0:T(128)S(6)} %copy.9.hot_ref, f32[2,128]{1,0:T(2,128)} %bitcast.29, bf16[128,4096]{1,0:T(8,128)(2,1)} %bitcast.25, ...), custom_call_target="tpu_custom_call" | custom-call | tf_op jit(solution)/shard_map/pallas_call | solution.py:247
  18.4 31.1 %all_to_all.20 = bf16[8,8,2048]{2,1,0:T(8,128)(2,1)S(1)} all-to-all(bf16[8,8,2048]{2,1,0:T(8,128)(2,1)S(1)} %get-tuple-element.9), channel_id=1, replica_groups={{0,16,32,48,64,80,96,112},{1,17,33,49,65,81,97,113},{2,18,34,50,66,82,9..., dimensions={0} | all-to-all | bytes 524288 | tf_op jit(solution)/shard_map/all_to_all | solution.py:273
  49.4 1.5 %shard_map.87 = bf16[8,64,2048]{2,1,0:T(8,128)(2,1)} custom-call(bf16[64,2048]{1,0:T(8,128)(2,1)S(1)} %bitcast.23), custom_call_target="tpu_custom_call" | custom-call | tf_op jit(solution)/shard_map/pallas_call | solution.py:247
  50.9 0.0 copy-start
  50.9 0.0 copy-start.3
  50.9 5.3 %all-to-all-start.1 = ((bf16[8,64,2048]{2,1,0:T(8,128)(2,1)}), bf16[8,64,2048]{2,1,0:T(8,128)(2,1)}, u32[]{:S(2)}, u32[]{:S(2)}) async-start(bf16[8,64,2048]{2,1,0:T(8,128)(2,1)} %shard_map.87), calls=%async_computation.1 | async-start | bytes 4194304 | tf_op jit(solution)/shard_map/all_to_all | solution.py:273
  56.2 0.0 copy-done
  56.2 0.0 copy-done.3
  56.2 0.0 copy-start.1
  56.2 0.0 copy-start.4
  56.2 0.1 pad_maximum_fusion
  56.3 2.1 %collective-permute-start.2 = (bf16[3,32,4096]{2,1,0:T(8,128)(2,1)S(1)}, bf16[3,32,4096]{2,1,0:T(8,128)(2,1)S(1)}, u32[]{:S(2)}, u32[]{:S(2)}) collective-permute-start(bf16[3,32,4096]{2,1,0:T(8,128)(2,1)S(1)} %pad_maximum_fusion), channel_id=1, source_target_pairs={{0,120},{1,121},{2,122},{3,123},{4,124},{5,125},{6,126},{7,127},{8... | collective-permute-start | bytes 2359304 | tf_op jit(solution)/shard_map/ppermute | solution.py:278
  58.4 3.5 %collective-permute-start.1 = (bf16[3,24,4096]{2,1,0:T(8,128)(2,1)S(1)}, bf16[3,24,4096]{2,1,0:T(8,128)(2,1)S(1)}, u32[]{:S(2)}, u32[]{:S(2)}) collective-permute-start(bf16[3,24,4096]{2,1,0:T(8,128)(2,1)S(1)} %pad_maximum_fusion.1), channel_id=1, source_target_pairs={{0,8},{1,9},{2,10},{3,11},{4,12},{5,13},{6,14},{7,15},{8,16},{9,17... | collective-permute-start | bytes 1769480 | tf_op jit(solution)/shard_map/ppermute | solution.py:278
  61.9 8.3 %collective-permute-done.1.below_ref = bf16[3,24,4096]{2,1,0:T(8,128)(2,1)S(1)} collective-permute-done((bf16[3,24,4096]{2,1,0:T(8,128)(2,1)S(1)}, bf16[3,24,4096]{2,1,0:T(8,128)(2,1)S(1)}, u32[]{:S(2)}, u32[]{:S(2)}) %collective-permute-start.1) | collective-permute-done | bytes 589856 | tf_op jit(solution)/shard_map/ppermute | solution.py:278
  70.2 0.0 collective-permute-done.2.above_ref
  70.2 0.0 copy-done.1
  70.2 0.0 copy-done.4
  70.2 0.2 shard_map.88.w_all
  70.4 0.9 all-to-all-done.1
  71.3 4.5 %shard_map.89 = bf16[8,528,128]{2,1,0:T(8,128)(2,1)S(1)} custom-call(bf16[512,2048]{1,0:T(8,128)(2,1)} %bitcast.8.rows_hbm, bf16[384,4096]{1,0:T(8,128)(2,1)S(1)} %shard_map.88.w_all), custom_call_target="tpu_custom_call" | custom-call | tf_op jit(solution)/shard_map/pallas_call | solution.py:247
  75.8 0.0 copy-start.2
  75.8 1.0 copy-done.2
  76.8 0.0 copy-start.5
  76.8 4.4 %all-to-all-start.2 = ((bf16[8,528,128]{2,1,0:T(8,128)(2,1)}), bf16[8,528,128]{2,1,0:T(8,128)(2,1)S(1)}, u32[]{:S(2)}, u32[]{:S(2)}) async-start(bf16[8,528,128]{2,1,0:T(8,128)(2,1)} %copy-done.2), calls=%async_computation.2 | async-start | bytes 2162688 | tf_op jit(solution)/shard_map/all_to_all | solution.py:273
  81.2 0.0 copy-done.5
  81.2 1.9 %collective-permute-start = (bf16[128,4096]{1,0:T(8,128)(2,1)S(1)}, bf16[128,4096]{1,0:T(8,128)(2,1)S(1)}, u32[]{:S(2)}, u32[]{:S(2)}) collective-permute-start(bf16[128,4096]{1,0:T(8,128)(2,1)S(1)} %bitcast.27), channel_id=1, source_target_pairs={{128,0},{256,128},{384,256},{129,1},{257,129},{385,257},{130,2},{2... | collective-permute-start | bytes 3145736 | tf_op jit(solution)/shard_map/ppermute | solution.py:285
  83.1 7.7 %all-to-all-done.2.got_ref = bf16[8,528,128]{2,1,0:T(8,128)(2,1)S(1)} async-done(((bf16[8,528,128]{2,1,0:T(8,128)(2,1)}), bf16[8,528,128]{2,1,0:T(8,128)(2,1)S(1)}, u32[]{:S(2)}, u32[]{:S(2)}) %all-to-all-start.2) | async-done | bytes 1081376 | tf_op jit(solution)/shard_map/all_to_all | solution.py:273
  90.8 0.9 shard_map.90
  91.7 17.6 %all_to_all.21.got_ref = bf16[8,72,128]{2,1,0:T(8,128)(2,1)S(1)} all-to-all(bf16[8,72,128]{2,1,0:T(8,128)(2,1)} %shard_map.90), channel_id=1, replica_groups={{0,16,32,48,64,80,96,112},{1,17,33,49,65,81,97,113},{2,18,34,50,66,82,9..., dimensions={0} | all-to-all | bytes 294912 | tf_op jit(solution)/shard_map/all_to_all | solution.py:273
  109.3 0.7 shard_map.91
  110.0 1.9 %collective-permute-start.3 = (bf16[8,1152]{1,0:T(8,128)(2,1)S(1)}, bf16[8,1152]{1,0:T(8,128)(2,1)S(1)}, u32[]{:S(2)}, u32[]{:S(2)}) collective-permute-start(bf16[8,1152]{1,0:T(8,128)(2,1)S(1)} %get-tuple-element.14), channel_id=1, source_target_pairs={{128,0},{256,128},{384,256},{129,1},{257,129},{385,257},{130,2},{2... | collective-permute-start | bytes 55304 | tf_op jit(solution)/shard_map/ppermute | solution.py:374
  111.9 0.0 collective-permute-done.cot_ref
  111.9 4.6 %collective-permute-done.3.moved_ref = bf16[8,1152]{1,0:T(8,128)(2,1)S(1)} collective-permute-done((bf16[8,1152]{1,0:T(8,128)(2,1)S(1)}, bf16[8,1152]{1,0:T(8,128)(2,1)S(1)}, u32[]{:S(2)}, u32[]{:S(2)}) %collective-permute-start.3) | collective-permute-done | bytes 18464 | tf_op jit(solution)/shard_map/ppermute | solution.py:374
  116.5 1.3 %shard_map.92 = bf16[128,4096]{1,0:T(8,128)(2,1)} custom-call(bf16[128,4096]{1,0:T(8,128)(2,1)S(1)} %collective-permute-done.cot_ref, bf16[8,1152]{1,0:T(8,128)(2,1)S(1)} %collective-permute-done.3.moved_ref), custom_call_target="tpu_custom_call" | custom-call | tf_op jit(solution)/shard_map/pallas_call | solution.py:247
  (1 shorter events, 0.0 us)
Async XLA Ops:
  50.9 5.3 %copy-start = (bf16[1,2,4096,56]{2,3,1,0:T(8,128)(2,1)S(1)}, bf16[1,2,4096,56]{2,3,1,0:T(8,128)(2,1)}, u32[]{:S(2)}) copy-start(bf16[1,2,4096,56]{2,3,1,0:T(8,128)(2,1)} %param.12) | copy-start | bytes 2752516
  50.9 5.3 %copy-start.3 = (bf16[1,56,4096]{2,1,0:T(8,128)(2,1)S(1)}, bf16[1,56,4096]{2,1,0:T(8,128)(2,1)}, u32[]{:S(2)}) copy-start(bf16[1,56,4096]{2,1,0:T(8,128)(2,1)} %param.13) | copy-start | bytes 1376260
  50.9 20.4 %all-to-all-start.1 = ((bf16[8,64,2048]{2,1,0:T(8,128)(2,1)}), bf16[8,64,2048]{2,1,0:T(8,128)(2,1)}, u32[]{:S(2)}, u32[]{:S(2)}) async-start(bf16[8,64,2048]{2,1,0:T(8,128)(2,1)} %shard_map.87), calls=%async_computation.1 | async-start | bytes 4194304 | tf_op jit(solution)/shard_map/all_to_all | solution.py:273
  56.2 14.0 %copy-start.1 = (bf16[1,2,4096,56]{2,3,1,0:T(8,128)(2,1)S(1)}, bf16[1,2,4096,56]{2,3,1,0:T(8,128)(2,1)}, u32[]{:S(2)}) copy-start(bf16[1,2,4096,56]{2,3,1,0:T(8,128)(2,1)} %param.12) | copy-start | bytes 2752516
  56.2 14.0 %copy-start.4 = (bf16[1,56,4096]{2,1,0:T(8,128)(2,1)S(1)}, bf16[1,56,4096]{2,1,0:T(8,128)(2,1)}, u32[]{:S(2)}) copy-start(bf16[1,56,4096]{2,1,0:T(8,128)(2,1)} %param.13) | copy-start | bytes 1376260
  56.3 14.0 %collective-permute-start.2 = (bf16[3,32,4096]{2,1,0:T(8,128)(2,1)S(1)}, bf16[3,32,4096]{2,1,0:T(8,128)(2,1)S(1)}, u32[]{:S(2)}, u32[]{:S(2)}) collective-permute-start(bf16[3,32,4096]{2,1,0:T(8,128)(2,1)S(1)} %pad_maximum_fusion), channel_id=1, source_target_pairs={{0,120},{1,121},{2,122},{3,123},{4,124},{5,125},{6,126},{7,127},{8... | collective-permute-start | bytes 2359304 | tf_op jit(solution)/shard_map/ppermute | solution.py:278
  58.4 11.8 %collective-permute-start.1 = (bf16[3,24,4096]{2,1,0:T(8,128)(2,1)S(1)}, bf16[3,24,4096]{2,1,0:T(8,128)(2,1)S(1)}, u32[]{:S(2)}, u32[]{:S(2)}) collective-permute-start(bf16[3,24,4096]{2,1,0:T(8,128)(2,1)S(1)} %pad_maximum_fusion.1), channel_id=1, source_target_pairs={{0,8},{1,9},{2,10},{3,11},{4,12},{5,13},{6,14},{7,15},{8,16},{9,17... | collective-permute-start | bytes 1769480 | tf_op jit(solution)/shard_map/ppermute | solution.py:278
  75.8 1.0 copy-start.2
  76.8 4.4 %copy-start.5 = (bf16[1,128,4096]{2,1,0:T(8,128)(2,1)S(1)}, bf16[1,128,4096]{2,1,0:T(8,128)(2,1)}, u32[]{:S(2)}) copy-start(bf16[1,128,4096]{2,1,0:T(8,128)(2,1)} %param.8) | copy-start | bytes 3145732
  76.8 14.0 %all-to-all-start.2 = ((bf16[8,528,128]{2,1,0:T(8,128)(2,1)}), bf16[8,528,128]{2,1,0:T(8,128)(2,1)S(1)}, u32[]{:S(2)}, u32[]{:S(2)}) async-start(bf16[8,528,128]{2,1,0:T(8,128)(2,1)} %copy-done.2), calls=%async_computation.2 | async-start | bytes 2162688 | tf_op jit(solution)/shard_map/all_to_all | solution.py:273
  81.2 30.7 %collective-permute-start = (bf16[128,4096]{1,0:T(8,128)(2,1)S(1)}, bf16[128,4096]{1,0:T(8,128)(2,1)S(1)}, u32[]{:S(2)}, u32[]{:S(2)}) collective-permute-start(bf16[128,4096]{1,0:T(8,128)(2,1)S(1)} %bitcast.27), channel_id=1, source_target_pairs={{128,0},{256,128},{384,256},{129,1},{257,129},{385,257},{130,2},{2... | collective-permute-start | bytes 3145736 | tf_op jit(solution)/shard_map/ppermute | solution.py:285
  110.0 6.6 %collective-permute-start.3 = (bf16[8,1152]{1,0:T(8,128)(2,1)S(1)}, bf16[8,1152]{1,0:T(8,128)(2,1)S(1)}, u32[]{:S(2)}, u32[]{:S(2)}) collective-permute-start(bf16[8,1152]{1,0:T(8,128)(2,1)S(1)} %get-tuple-element.14), channel_id=1, source_target_pairs={{128,0},{256,128},{384,256},{129,1},{257,129},{385,257},{130,2},{2... | collective-permute-start | bytes 55304 | tf_op jit(solution)/shard_map/ppermute | solution.py:374
